TPU v7x, 512 devices: a whole 4x8x8 slice. The times are simulated.
512 devices in a mesh: seq: 64 (over y, x, core), head: 8 (over z).
Axes of the slice: x: 4, y: 8, z: 8, core: 2. Of those that a mesh axis runs over, the one named last changes fastest.
Arguments:
- queries: bfloat16 [16384, 4096], P('seq', 'head'), may hold values from -6 to 6
- key_rows: bfloat16 [16384, 4096], P('seq', 'head'), may hold values from -6 to 6
- values: bfloat16 [16384, 4096], P('seq', 'head'), may hold values from -12 to 12
- cotangent: bfloat16 [16384, 4096], P('seq', 'head'), may hold values from -12 to 12
- carried_state: float32 [32, 128, 128], P('head'), may hold values from -192 to 192
- norm_gain: float32 [4096], P('head'), may hold values from 0.25 to 1.75
Outputs:
- attended: bfloat16 [16384, 4096], P('seq', 'head')
- gradient_queries: bfloat16 [16384, 4096], P('seq', 'head')
- gradient_keys: bfloat16 [16384, 4096], P('seq', 'head')
- grad_value: bfloat16 [16384, 4096], P('seq', 'head')
- grad_state: float32 [32, 128, 128], P('head')
- grad_gain: float32 [4096], P('head')
All inputs are finite; a program needn't handle non-finite values.
Results may differ from a plain program's by a relative error of at most 0.0065.
Values may be sent and summed in bfloat16 or wider, within the bound.
A program may use at most 64 MiB of HBM per device.

v0:
```python
import jax
import jax.numpy as jnp
from jax import lax
from jax.sharding import PartitionSpec as P

EPS = 1e-05


def prefix(x, axis, combine, identity, reverse):
    count, mine = (lax.axis_size(axis), lax.axis_index(axis))
    everything = lax.all_gather(x, axis)
    start = jnp.broadcast_to(jnp.asarray(identity, x.dtype), x.shape)

    def lap(k, before):
        at = count - 1 - k if reverse else k
        reached = at > mine if reverse else at < mine
        new = combine(before, everything[at])
        return jnp.where(reached, new, before)

    return lax.fori_loop(0, count, lap, start)


def add_states(earlier, later):
    return earlier + later


def chain_rounded(states, offset, reverse):
    summed = prefix(states, "seq", add_states, jnp.zeros_like(states), reverse)
    return (offset + summed).astype(jnp.bfloat16)


def on_device(queries, key_rows, values, cotangent, carried_state, norm_gain):
    length, width = queries.shape
    heads = carried_state.shape[0]
    head_dim = carried_state.shape[1]
    total_width = width * lax.axis_size("head")
    head_queries = queries.reshape(length, heads, head_dim)
    head_keys = key_rows.reshape(length, heads, head_dim)
    head_values = values.reshape(length, heads, head_dim)
    causal_mask = jnp.arange(length)[:, None] >= jnp.arange(length)[None, :]
    gain_heads = norm_gain.reshape(heads, head_dim)
    local_state = jnp.einsum(
        "lhd,lhe->hde", head_keys, head_values, preferred_element_type=jnp.float32
    )
    preceding_part = chain_rounded(local_state, carried_state, False)
    score_matrix = jnp.einsum(
        "ftz,ytz->tfy", head_queries, head_keys, preferred_element_type=jnp.float32
    )
    score_matrix = jnp.where(causal_mask, score_matrix, jnp.float32(0.0)).astype(jnp.bfloat16)
    unnormed = jnp.einsum(
        "hlm,mhe->lhe", score_matrix, head_values, preferred_element_type=jnp.float32
    )
    unnormed = unnormed + jnp.einsum(
        "lhd,hde->lhe", head_queries, preceding_part, preferred_element_type=jnp.float32
    )
    cot_wide = cotangent.reshape(length, heads, head_dim).astype(jnp.float32)
    scaled = cot_wide * gain_heads
    square_part = jnp.sum(unnormed * unnormed, axis=(1, 2))
    dot_part = jnp.sum(scaled * unnormed, axis=(1, 2))
    square_sum, dot_sum = lax.psum((square_part, dot_part), "head")
    norm_scale = jnp.sqrt(square_sum / total_width + EPS)[:, None, None]
    normed = unnormed / norm_scale
    attended = (gain_heads * normed).astype(jnp.bfloat16).reshape(length, width)
    grad_unnormed = (
        (scaled - normed * (dot_sum[:, None, None] / (total_width * norm_scale))) / norm_scale
    ).astype(jnp.bfloat16)
    gain_part = jnp.sum(cot_wide * normed, axis=0).reshape(width)
    grad_local = jnp.einsum(
        "lhd,lhe->hde", head_queries, grad_unnormed, preferred_element_type=jnp.float32
    )
    following_part = chain_rounded(grad_local, jnp.zeros_like(grad_local), True)
    grad_state, grad_gain = lax.psum((grad_local, gain_part), "seq")
    blended_output = jnp.einsum(
        "lhe,mhe->hlm", grad_unnormed, head_values, preferred_element_type=jnp.float32
    )
    blended_output = jnp.where(causal_mask, blended_output, jnp.float32(0.0)).astype(jnp.bfloat16)
    gradient_queries = jnp.einsum(
        "krx,xkn->rkn", blended_output, head_keys, preferred_element_type=jnp.float32
    )
    gradient_queries = gradient_queries + jnp.einsum(
        "xif,iuf->xiu", grad_unnormed, preceding_part, preferred_element_type=jnp.float32
    )
    gradient_keys = jnp.einsum(
        "nox,ony->xny", blended_output, head_queries, preferred_element_type=jnp.float32
    )
    gradient_keys = gradient_keys + jnp.einsum(
        "yon,otn->yot", head_values, following_part, preferred_element_type=jnp.float32
    )
    grad_value = jnp.einsum(
        "nou,onk->unk", score_matrix, grad_unnormed, preferred_element_type=jnp.float32
    )
    grad_value = grad_value + jnp.einsum(
        "klj,ljr->klr", head_keys, following_part, preferred_element_type=jnp.float32
    )
    return (
        attended,
        gradient_queries.astype(jnp.bfloat16).reshape(length, width),
        gradient_keys.astype(jnp.bfloat16).reshape(length, width),
        grad_value.astype(jnp.bfloat16).reshape(length, width),
        grad_state,
        grad_gain,
    )


def solution(mesh):
    in_specs = (
        P("seq", "head"),
        P("seq", "head"),
        P("seq", "head"),
        P("seq", "head"),
        P("head", None, None),
        P("head"),
    )
    out_specs = (
        P("seq", "head"),
        P("seq", "head"),
        P("seq", "head"),
        P("seq", "head"),
        P("head", None, None),
        P("head"),
    )
    return jax.shard_map(
        on_device, mesh=mesh, in_specs=in_specs, out_specs=out_specs, check_vma=False
    )
```

profile of v0, /device:TPU:1, one launch (start us, length us, event | category | flops | bytes accessed | tf_op | source)
XLA Modules:
  0.0 599.0 jit_solution(11291634717412541404)
XLA Ops:
  7.3 1.2 copy.105
  8.5 1.9 fusion.11
  10.4 1.1 copy.42
  11.5 1.3 fusion
  12.8 1.3 convolution_bitcast_fusion.5
  14.1 108.1 %all-gather.5.cloned.1.call-done = f32[256,128,128]{2,1,0:T(8,128)} async-done(((f32[4,128,128]{2,1,0:T(8,128)}), f32[256,128,128]{2,1,0:T(8,128)}) %all-gather.5.cloned.1.call-update) | async-done | bytes 16777232 | tf_op jit(solution)/shard_map/all_gather | solution.py:11
  122.2 68.1 %while.30 = (s32[]{:T(128)}, f32[4,128,128]{2,1,0:T(8,128)S(1)}, s32[]{:T(128)}, f32[64,4,128,128]{3,2,1,0:T(8,128)}, s32[]{:T(128)}, /*index=5*/s32[]{:T(128)}) while((s32[]{:T(128)}, f32[4,128,128]{2,1,0:T(8,128)S(1)}, s32[]{:T(128)}, f32[64,4,128,128]{3,2,1,0:T(8,128)}, s32[]{:T(128)}, /*index=5*/s32[]{:T(128)}) %tuple.90), condition=%wide.region_1.2_spmd.clone, body=%wide.region_0.1_spmd.clone.sunk | while | flops 196612 | bytes 786533 | solution.py:20
  123.2 1.0 add_select_fusion.4
  124.3 1.0 add_select_fusion.4
  125.4 1.0 add_select_fusion.4
  126.4 1.0 add_select_fusion.4
  127.5 1.0 add_select_fusion.4
  128.6 1.0 add_select_fusion.4
  129.6 1.0 add_select_fusion.4
  130.7 1.0 add_select_fusion.4
  131.8 1.0 add_select_fusion.4
  132.8 1.0 add_select_fusion.4
  133.9 1.0 add_select_fusion.4
  134.9 1.0 add_select_fusion.4
  136.0 1.0 add_select_fusion.4
  137.1 1.0 add_select_fusion.4
  138.1 1.0 add_select_fusion.4
  139.2 1.0 add_select_fusion.4
  147.7 1.0 add_select_fusion.4
  149.8 1.0 add_select_fusion.4
  152.0 1.0 add_select_fusion.4
  154.1 1.0 add_select_fusion.4
  156.2 1.0 add_select_fusion.4
  158.4 1.0 add_select_fusion.4
  167.9 1.0 add_select_fusion.4
  170.1 1.0 add_select_fusion.4
  172.2 1.0 add_select_fusion.4
  174.3 1.0 add_select_fusion.4
  176.5 1.0 add_select_fusion.4
  178.6 1.0 add_select_fusion.4
  188.2 1.0 add_select_fusion.4
  191.6 14.4 %psum.28 = f32[256]{0:T(256)S(1)} all-reduce(f32[256]{0:T(256)S(1)} %get-tuple-element.263), channel_id=1, replica_groups=mesh['seq'=64,'head'=8] {'head'}, use_global_device_ids=true, to_apply=%region_3.4 | all-reduce | flops 256 | bytes 2048 | tf_op jit(solution)/shard_map/psum | solution.py:60
  206.9 11.1 %psum.29 = f32[256]{0:T(256)S(1)} all-reduce(f32[256]{0:T(256)S(1)} %get-tuple-element.244), channel_id=1, replica_groups=mesh['seq'=64,'head'=8] {'head'}, use_global_device_ids=true, to_apply=%region_5.6 | all-reduce | flops 256 | bytes 2048 | tf_op jit(solution)/shard_map/psum | solution.py:60
  222.4 1.2 fusion.1
  224.9 131.5 %psum.31 = f32[512]{0:T(512)} all-reduce(f32[512]{0:T(512)S(1)} %bitcast.127), channel_id=1, replica_groups=mesh['seq'=64,'head'=8] {'seq'}, use_global_device_ids=true, to_apply=%region_10.11 | all-reduce | flops 512 | bytes 4096 | tf_op jit(solution)/shard_map/psum | solution.py:72
  356.9 58.7 %all-reduce.2.cloned.1.call-done = f32[4,128,128]{1,2,0:T(8,128)} async-done(((f32[4,128,128]{1,2,0:T(8,128)}), f32[4,128,128]{1,2,0:T(8,128)}) %all-reduce.2.cloned.1.call-update) | async-done | bytes 262160 | tf_op jit(solution)/shard_map/psum | solution.py:72
  415.7 1.8 copy.57
  417.4 104.4 %all-gather.7.cloned.1.call-done = f32[256,128,128]{2,1,0:T(8,128)} async-done(((f32[4,128,128]{2,1,0:T(8,128)}), f32[256,128,128]{2,1,0:T(8,128)}) %all-gather.7.cloned.1.call-update) | async-done | bytes 16777232 | tf_op jit(solution)/shard_map/all_gather | solution.py:11
  521.9 68.4 %while.31 = (s32[]{:T(128)}, f32[4,128,128]{2,1,0:T(8,128)S(1)}, s32[]{:T(128)}, f32[64,4,128,128]{3,2,1,0:T(8,128)}, s32[]{:T(128)}, /*index=5*/s32[]{:T(128)}, s32[]{:T(128)}, s32[]{:T(128)}) while((s32[]{:T(128)}, f32[4,128,128]{2,1,0:T(8,128)S(1)}, s32[]{:T(128)}, f32[64,4,128,128]{3,2,1,0:T(8,128)}, s32[]{:T(128)}, ...), condition=%wide.region_7.8_spmd.clone, body=%wide.region_6.7_spmd.clone.sunk | while | flops 196616 | bytes 786595 | solution.py:20
  525.1 1.0 add_select_fusion.5
  528.3 1.0 add_select_fusion.5
  530.4 1.0 add_select_fusion.5
  533.6 1.0 add_select_fusion.5
  536.8 1.0 add_select_fusion.5
  542.2 1.0 add_select_fusion.5
  545.4 1.0 add_select_fusion.5
  548.6 1.0 add_select_fusion.5
  550.7 1.0 add_select_fusion.5
  553.9 1.0 add_select_fusion.5
  557.1 1.0 add_select_fusion.5
  562.5 1.0 add_select_fusion.5
  565.7 1.0 add_select_fusion.5
  568.9 1.0 add_select_fusion.5
  571.0 1.0 add_select_fusion.5
  574.2 1.0 add_select_fusion.5
  577.4 1.0 add_select_fusion.5
  582.8 1.0 add_select_fusion.5
  586.0 1.0 add_select_fusion.5
  589.2 1.0 add_select_fusion.5
  (116 shorter events, 92.8 us)
Async XLA Ops:
  7.2 4.3 copy-start
  7.2 583.1 %copy-start.3 = (bf16[256,512]{1,0:T(8,128)(2,1)S(1)}, bf16[256,512]{1,0:T(8,128)(2,1)}, u32[]{:S(2)}) copy-start(bf16[256,512]{1,0:T(8,128)(2,1)} %param.11) | copy-start | bytes 786436
  7.2 215.2 %copy-start.1 = (bf16[256,512]{1,0:T(8,128)(2,1)S(1)}, bf16[256,512]{1,0:T(8,128)(2,1)}, u32[]{:S(2)}) copy-start(bf16[256,512]{1,0:T(8,128)(2,1)} %param.12) | copy-start | bytes 786436
  7.2 115.0 %all-gather.5.cloned.1.call-start = ((), (), s32[]{:S(2)}) async-start(), calls=%async_computation.1 | async-start | bytes 17039360 | tf_op jit(solution)/shard_map/all_gather | solution.py:11
  11.5 178.8 %copy-start.4 = (pred[256,256]{1,0:T(8,128)(4,1)}, pred[256,256]{1,0:T(8,128)(4,1)S(1)}, u32[]{:S(2)}) copy-start(pred[256,256]{1,0:T(8,128)(4,1)S(1)} %iota_compare_fusion) | copy-start | bytes 196612
  219.2 0.9 copy-start.2
  220.0 195.6 %all-reduce.2.cloned.1.call-start = ((), (), s32[]{:S(2)}) async-start(), calls=%async_computation | async-start | bytes 524288 | tf_op jit(solution)/shard_map/psum | solution.py:72
  220.8 301.1 %all-gather.7.cloned.1.call-start = ((), (), s32[]{:S(2)}) async-start(), calls=%async_computation.2 | async-start | bytes 17039360 | tf_op jit(solution)/shard_map/all_gather | solution.py:11
Sparse Core Ops, SparseCore 0:
  11.9 110.1 all-gather.4
  224.9 190.7 all-reduce.1
  419.6 102.2 all-gather.6
where the time goes:
time: 603 us; the launch traced here: 599 us
  waiting for transfers between devices  273 us (45%)
  blocking collectives  157 us (26%)
  other arithmetic  136 us (23%)
  between operations  13.9 us (2%)
  local copies, waits for them, and re-layouts  8.33 us (1%)
  matrix products  7.61 us (1%)
    all_gather x2, waiting for transfers between devices, prefix(): everything = lax.all_gather(x, axis)  213 us
    select_n x128, other arithmetic, lap(): return jnp.where(reached, new, before)  133 us
    psum x1, blocking collectives, on_device(): grad_state, grad_gain = lax.psum((grad_local, gain_part), 'seq')  132 us
    psum x1, waiting for transfers between devices, on_device(): grad_state, grad_gain = lax.psum((grad_local, gain_part), 'seq')  58.7 us
    psum x2, blocking collectives, on_device(): square_sum, dot_sum = lax.psum((square_part, dot_part), 'head')  25.6 us
  transfers between devices with their start and end apart: 3, of which 3 were waited for; matrix products, arithmetic and copies ran while one was open for 2% of the time, Pallas kernels for 0%

commit v1 on v0

v1 whole, which is shorter than its diff:
```python
import jax
import jax.numpy as jnp
from jax import lax
from jax.experimental import pallas as pl
from jax.experimental.pallas import tpu as pltpu
from jax.sharding import PartitionSpec as P

EPS = 1e-05
MESH = pl.DeviceIdType.MESH
F32 = jnp.float32
BF16 = jnp.bfloat16
ROW = 8
COL = 8
NZ = 8
HEADS = 4
D = 128
L = 256
WIDTH = HEADS * D
TOTAL_WIDTH = WIDTH * NZ
HALF = D // 2


def nn(a, b):
    return lax.dot_general(a, b, (((1,), (0,)), ((), ())), preferred_element_type=F32)


def nt(a, b):
    return lax.dot_general(a, b, (((1,), (1,)), ((), ())), preferred_element_type=F32)


def tn(a, b):
    return lax.dot_general(a, b, (((0,), (0,)), ((), ())), preferred_element_type=F32)


def comm_kernel(
    q_hbm, k_hbm, v_hbm, c_hbm, carry_hbm, gain_hbm,
    att_o, gq_o, gkp_o, gvp_o, suf_o, tot_o, gg_o,
    q, k, v, c, carry, gain,
    sb, rb, cb, ps, pre,
    sb2, rb2, cb2, ps2, suf, tot,
    zb, grow, gcol,
    sc_t, un, gu, att, gq, gkp, gvp, gg,
    in_sem, out_sem, send_sem, recv_sem,
):
    seq = lax.axis_index("seq")
    z = lax.axis_index("head")
    y = seq // ROW
    me = seq % ROW
    base = y * ROW

    def row_dev(kk):
        return (base + lax.rem(me + kk, ROW), z)

    def col_dev(kk):
        return (lax.rem(y + kk, COL) * ROW + me, z)

    def z_dev(kk):
        return (seq, lax.rem(z + kk, NZ))

    barrier = pltpu.get_barrier_semaphore()
    for dev, count in ((row_dev, ROW), (col_dev, COL), (z_dev, NZ)):
        for kk in range(1, count):
            pl.semaphore_signal(barrier, inc=1, device_id=dev(kk), device_id_type=MESH)

    loads = []
    for i, (src, dst) in enumerate(
        ((k_hbm, k), (v_hbm, v), (q_hbm, q), (c_hbm, c), (carry_hbm.at[me], carry), (gain_hbm, gain))
    ):
        load = pltpu.make_async_copy(src, dst, in_sem.at[i])
        load.start()
        loads.append(load)

    pending = []

    def exchange(stage, dev, count, src_of, dst, mine):
        copies = []
        for kk in range(1, count):
            target = lax.rem(mine + kk, count)
            copy = pltpu.make_async_remote_copy(
                src_ref=src_of(target),
                dst_ref=dst.at[mine],
                send_sem=send_sem.at[stage, kk],
                recv_sem=recv_sem.at[stage, kk],
                device_id=dev(kk),
                device_id_type=MESH,
            )
            copy.start()
            copies.append(copy)
        pending.extend(copies)

        def wait():
            for kk in range(1, count):
                origin = lax.rem(mine + count - kk, count)
                pltpu.make_async_remote_copy(
                    src_ref=src_of(origin),
                    dst_ref=dst.at[origin],
                    send_sem=send_sem.at[stage, kk],
                    recv_sem=recv_sem.at[stage, kk],
                    device_id=dev(kk),
                    device_id_type=MESH,
                ).wait_recv()

        return wait

    def head(ref, h):
        return ref[:, h * D:(h + 1) * D]

    rows = lax.broadcasted_iota(jnp.int32, (L, L), 0)
    cols = lax.broadcasted_iota(jnp.int32, (L, L), 1)
    lower = rows >= cols
    upper = rows <= cols

    loads[0].wait()
    loads[1].wait()
    for h in range(HEADS):
        state = tn(head(k, h), head(v, h)).astype(BF16)
        sb[2 * h] = state[:HALF]
        sb[2 * h + 1] = state[HALF:]
    pl.semaphore_wait(barrier, ROW + COL + NZ - 3)
    wait_a = exchange(0, row_dev, ROW, lambda t: sb.at[t], rb, me)
    rb[me] = sb[me]

    loads[2].wait()
    for h in range(HEADS):
        score = jnp.where(lower, nt(head(q, h), head(k, h)), 0.0).astype(BF16)
        un[h] = nn(score, head(v, h))

    wait_a()
    acc = rb[0].astype(F32)
    for r in range(1, ROW):
        acc = acc + rb[r].astype(F32)
    cb[y] = acc.astype(BF16)
    wait_b = exchange(1, col_dev, COL, lambda t: cb.at[y], cb, y)

    for h in range(HEADS):
        sc_t[h] = jnp.where(upper, nt(head(k, h), head(q, h)), 0.0).astype(BF16)
    loads[3].wait()
    loads[4].wait()
    loads[5].wait()

    wait_b()
    acc = carry[...]
    for r in range(COL):
        acc = acc + jnp.where(r < y, cb[r].astype(F32), 0.0)
    for r in range(ROW):
        ps[r] = acc.astype(BF16)
        if r < ROW - 1:
            acc = acc + rb[r].astype(F32)
    wait_c = exchange(2, row_dev, ROW, lambda t: ps.at[t], pre, me)
    pre[me] = ps[me]
    wait_c()

    square = jnp.zeros((L, D), F32)
    dots = jnp.zeros((L, D), F32)
    for h in range(HEADS):
        u = un[h] + nn(head(q, h), pre[2 * h:2 * h + 2].reshape(D, D))
        un[h] = u
        square = square + u * u
        dots = dots + head(c, h).astype(F32) * head(gain, h) * u

    def lane_sum(x):
        return jnp.sum(x.T, axis=0, keepdims=True)

    tile_row = lax.broadcasted_iota(jnp.int32, (8, D), 0)
    parts = (lane_sum(square[:D]), lane_sum(square[D:]), lane_sum(dots[:D]), lane_sum(dots[D:]))
    tile = jnp.zeros((8, D), F32)
    for i, part in enumerate(parts):
        tile = jnp.where(tile_row == i, part, tile)
    zb[z] = tile
    wait_z = exchange(3, z_dev, NZ, lambda t: zb.at[z], zb, z)
    wait_z()
    sums = zb[0]
    for i in range(1, NZ):
        sums = sums + zb[i]
    mean = sums[0:2] / TOTAL_WIDTH + EPS
    inverse = 1.0 / jnp.sqrt(mean)
    factor = sums[2:4] / (TOTAL_WIDTH * mean)
    both = jnp.concatenate([inverse, factor, jnp.zeros((4, D), F32)], axis=0).T
    inv_col = jnp.concatenate([both[:, 0:1], both[:, 1:2]], axis=0)
    fac_col = jnp.concatenate([both[:, 2:3], both[:, 3:4]], axis=0)
    inv_col = jnp.broadcast_to(inv_col, (L, D))
    fac_col = jnp.broadcast_to(fac_col, (L, D))

    grow[me] = jnp.zeros((8, D), F32)
    for h in range(HEADS):
        cot = head(c, h).astype(F32)
        g = ((cot * head(gain, h) - un[h] * fac_col) * inv_col).astype(BF16)
        gu[h] = g
        state = tn(head(q, h), g).astype(BF16)
        sb2[2 * h] = state[:HALF]
        sb2[2 * h + 1] = state[HALF:]
    wait_a = exchange(4, row_dev, ROW, lambda t: sb2.at[t], rb2, me)
    rb2[me] = sb2[me]

    for h in range(HEADS):
        normed = un[h] * inv_col
        att[:, h * D:(h + 1) * D] = (normed * head(gain, h)).astype(BF16)
        part = jnp.sum(head(c, h).astype(F32) * normed, axis=0, keepdims=True)
        grow[me, h:h + 1] = part
    wait_g = exchange(5, row_dev, ROW, lambda t: grow.at[me], grow, me)
    out_att = pltpu.make_async_copy(att, att_o, out_sem.at[0])
    out_att.start()

    for h in range(HEADS):
        mixed = jnp.where(lower, nt(gu[h], head(v, h)), 0.0).astype(BF16)
        gq[:, h * D:(h + 1) * D] = (
            nn(mixed, head(k, h)) + nt(gu[h], pre[2 * h:2 * h + 2].reshape(D, D))
        ).astype(BF16)
    out_gq = pltpu.make_async_copy(gq, gq_o, out_sem.at[1])
    out_gq.start()

    wait_a()
    acc = rb2[0].astype(F32)
    for r in range(1, ROW):
        acc = acc + rb2[r].astype(F32)
    cb2[y] = acc.astype(BF16)
    wait_b = exchange(6, col_dev, COL, lambda t: cb2.at[y], cb2, y)
    wait_g()
    gsum = grow[0]
    for r in range(1, ROW):
        gsum = gsum + grow[r]
    gcol[y] = gsum
    wait_g = exchange(7, col_dev, COL, lambda t: gcol.at[y], gcol, y)

    for h in range(HEADS):
        mixed_t = jnp.where(upper, nt(head(v, h), gu[h]), 0.0).astype(BF16)
        gkp[:, h * D:(h + 1) * D] = nn(mixed_t, head(q, h))
        gvp[:, h * D:(h + 1) * D] = nn(sc_t[h], gu[h])
    out_gk = pltpu.make_async_copy(gkp, gkp_o, out_sem.at[2])
    out_gk.start()
    out_gv = pltpu.make_async_copy(gvp, gvp_o, out_sem.at[3])
    out_gv.start()

    wait_b()
    total = cb2[0].astype(F32)
    acc = jnp.zeros((HALF, D), F32)
    for r in range(COL):
        part = cb2[r].astype(F32)
        if r:
            total = total + part
        acc = acc + jnp.where(r > y, part, 0.0)
    for r in range(ROW - 1, -1, -1):
        ps2[r] = acc.astype(BF16)
        if r:
            acc = acc + rb2[r].astype(F32)
    wait_c = exchange(8, row_dev, ROW, lambda t: ps2.at[t], suf, me)
    tot[me] = total.astype(BF16)
    wait_t = exchange(9, row_dev, ROW, lambda t: tot.at[me], tot, me)
    suf[me] = ps2[me]
    wait_g()
    gsum = gcol[0]
    for r in range(1, COL):
        gsum = gsum + gcol[r]
    gg[...] = gsum
    out_gg = pltpu.make_async_copy(gg, gg_o, out_sem.at[4])
    out_gg.start()
    wait_c()
    out_suf = pltpu.make_async_copy(suf, suf_o, out_sem.at[5])
    out_suf.start()
    wait_t()
    out_tot = pltpu.make_async_copy(tot, tot_o, out_sem.at[6])
    out_tot.start()
    for copy in pending:
        copy.wait_send()
    for copy in (out_att, out_gq, out_gk, out_gv, out_gg, out_suf, out_tot):
        copy.wait()


def tail_kernel(k, v, att_i, gq_i, gkp, gvp, suf, tot, gg, att, gq, gk, gv, gs, gain):
    att[...] = att_i[...]
    gq[...] = gq_i[...]
    for h in range(HEADS):
        lanes = slice(h * D, (h + 1) * D)
        suffix = suf[2 * h:2 * h + 2].reshape(D, D)
        gk[:, lanes] = (gkp[:, lanes] + nt(v[:, lanes], suffix)).astype(BF16)
        gv[:, lanes] = (gvp[:, lanes] + nn(k[:, lanes], suffix)).astype(BF16)
        gain[:, lanes] = gg[h:h + 1]
    gs[...] = tot[...].astype(F32)


def on_device(queries, key_rows, values, cotangent, carried_state, norm_gain):
    any_spec = pl.BlockSpec(memory_space=pl.ANY)
    vmem_spec = pl.BlockSpec(memory_space=pltpu.VMEM)
    wide = (L, WIDTH)
    slices = (ROW, HALF, D)
    sds = jax.ShapeDtypeStruct
    att, gq, gkp, gvp, suf, tot, gg = pl.pallas_call(
        comm_kernel,
        out_shape=(
            sds(wide, BF16), sds(wide, BF16), sds(wide, F32), sds(wide, F32),
            sds(slices, BF16), sds(slices, BF16), sds((8, D), F32),
        ),
        in_specs=[any_spec] * 6,
        out_specs=[any_spec] * 7,
        scratch_shapes=[
            pltpu.VMEM(wide, BF16), pltpu.VMEM(wide, BF16), pltpu.VMEM(wide, BF16), pltpu.VMEM(wide, BF16),
            pltpu.VMEM((HALF, D), F32), pltpu.VMEM((1, WIDTH), F32),
            *[pltpu.VMEM(slices, BF16)] * 5,
            *[pltpu.VMEM(slices, BF16)] * 6,
            pltpu.VMEM((NZ, 8, D), F32), pltpu.VMEM((ROW, 8, D), F32), pltpu.VMEM((COL, 8, D), F32),
            pltpu.VMEM((HEADS, L, L), BF16), pltpu.VMEM((HEADS, L, D), F32), pltpu.VMEM((HEADS, L, D), BF16),
            pltpu.VMEM(wide, BF16), pltpu.VMEM(wide, BF16), pltpu.VMEM(wide, F32), pltpu.VMEM(wide, F32),
            pltpu.VMEM((8, D), F32),
            pltpu.SemaphoreType.DMA((6,)), pltpu.SemaphoreType.DMA((7,)),
            pltpu.SemaphoreType.DMA((10, 8)), pltpu.SemaphoreType.DMA((10, 8)),
        ],
        compiler_params=pltpu.CompilerParams(collective_id=0, has_side_effects=True),
        name="scan_comm",
    )(queries, key_rows, values, cotangent, carried_state.reshape(slices), norm_gain.reshape(1, WIDTH))
    att, gq, gk, gv, gs, gain = pl.pallas_call(
        tail_kernel,
        out_shape=(
            sds(wide, BF16), sds(wide, BF16), sds(wide, BF16), sds(wide, BF16),
            sds(slices, F32), sds((1, WIDTH), F32),
        ),
        in_specs=[vmem_spec] * 9,
        out_specs=[vmem_spec] * 6,
        name="tail",
    )(key_rows, values, att, gq, gkp, gvp, suf, tot, gg)
    return att, gq, gk, gv, gs.reshape(HEADS, D, D), gain.reshape(WIDTH)


def solution(mesh):
    in_specs = (
        P("seq", "head"),
        P("seq", "head"),
        P("seq", "head"),
        P("seq", "head"),
        P("head", None, None),
        P("head"),
    )
    out_specs = (
        P("seq", "head"),
        P("seq", "head"),
        P("seq", "head"),
        P("seq", "head"),
        P("head", None, None),
        P("head"),
    )
    return jax.shard_map(
        on_device, mesh=mesh, in_specs=in_specs, out_specs=out_specs, check_vma=False
    )
```

time: 603 us -> 56.1 us (0.09)
  waiting for transfers between devices: 273 us -> 0 us
  blocking collectives: 157 us -> 0 us
  other arithmetic: 136 us -> 0 us
  Pallas kernels: 0 us -> 55.3 us
  between operations: 13.9 us -> 0.64 us
  local copies, waits for them, and re-layouts: 8.33 us -> 0 us
  matrix products: 7.61 us -> 0 us
    all_gather x2 -> x0, waiting for transfers between devices: 213 us -> none  [prefix(): everything = lax.all_gather(x, axis)]
    psum x3 -> x0, blocking collectives: 157 us -> none  [the longest x1 132 us: on_device(): grad_state, grad_gain = lax.psum((grad_local, gain_part), 'seq')]
    select_n x128 -> x0, other arithmetic: 133 us -> none  [lap(): return jnp.where(reached, new, before)]
    psum x1 -> x0, waiting for transfers between devices: 58.7 us -> none  [on_device(): grad_state, grad_gain = lax.psum((grad_local, gain_part), 'seq')]
    pallas_call x0 -> x2, Pallas kernels: none -> 55.3 us  [the longest x1 52.4 us: on_device(): pl.pallas_call(comm_kernel, out_shape=(sds(wide, BF16), sds(wide, BF16),...]
    dot_general x12 -> x0, matrix products: 7.61 us -> none  [the longest x1 1.87 us: on_device(): jnp.einsum('lhd,lhe->hde', head_keys, head_values, preferred_element_type...]
  transfers between devices with their start and end apart: 3 -> 0, of which waited for: 3 -> 0; matrix products, arithmetic and copies ran while one was open for 2% -> 0% of each run, Pallas kernels for 0% -> 0%
where the time goes in v1:
time: 56.1 us; the launch traced here: 55.9 us
  Pallas kernels  55.3 us (99%)
  between operations  0.64 us (1%)
    pallas_call x1, Pallas kernels, on_device(): pl.pallas_call(comm_kernel, out_shape=(sds(wide, BF16), sds(wide, BF16),...  52.4 us
    pallas_call x1, Pallas kernels, on_device(): pl.pallas_call(tail_kernel, out_shape=(sds(wide, BF16), sds(wide, BF16),...  2.88 us

profile of v1, /device:TPU:1, one launch (start us, length us, event | category | flops | bytes accessed | tf_op | source)
XLA Modules:
  0.0 55.9 jit_solution(5762507315351595441)
XLA Ops:
  0.6 52.4 %scan_comm.1 = (bf16[256,512]{1,0:T(8,128)(2,1)}, bf16[256,512]{1,0:T(8,128)(2,1)}, f32[256,512]{1,0:T(8,128)}, f32[256,512]{1,0:T(8,128)}, bf16[8,64,128]{2,1,0...) custom-call(bf16[256,512]{1,0:T(8,128)(2,1)} %q_hbm.1, bf16[256,512]{1,0:T(8,128)(2,1)} %k.1, ...), custom_call_target="tpu_custom_call" | custom-call | tf_op jit(solution)/shard_map/scan_comm/pallas_call | solution.py:287
  53.0 2.9 %tail.1 = (bf16[256,512]{1,0:T(8,128)(2,1)}, bf16[256,512]{1,0:T(8,128)(2,1)}, bf16[256,512]{1,0:T(8,128)(2,1)}, bf16[256,512]{1,0:T(8,128)(2,1)}, f32[8,64,128]{2,1,0:T(8,128)}, /*index=5*/f32[1,512]{1,0:T(1,128)}) custom-call(bf16[256,512]{1,0:T(8,128)(2,1)} %k.1, bf16[256,512]{1,0:T(8,128)(2,1)} %v.1, bf16[256,512]{1,0:T(8,128)(2,1)} %get-tuple-element.19.att_i, ...), custom_call_target="tpu_custom_call" | custom-call | tf_op jit(solution)/shard_map/tail/pallas_call | solution.py:310

commit v2 on v1

v2 whole, which is shorter than its diff:
```python
import jax
import jax.numpy as jnp
from jax import lax
from jax.experimental import pallas as pl
from jax.experimental.pallas import tpu as pltpu
from jax.sharding import PartitionSpec as P

EPS = 1e-05
MESH = pl.DeviceIdType.MESH
F32 = jnp.float32
BF16 = jnp.bfloat16
ROW = 8
COL = 8
NZ = 8
HEADS = 4
D = 128
L = 256
WIDTH = HEADS * D
TOTAL_WIDTH = WIDTH * NZ
HALF = D // 2
CHUNKS = 1
PIECE = HALF // CHUNKS
FAR_FIRST = (4, 3, 5, 2, 6, 1, 7)


def nn(a, b):
    return lax.dot_general(a, b, (((1,), (0,)), ((), ())), preferred_element_type=F32)


def nt(a, b):
    return lax.dot_general(a, b, (((1,), (1,)), ((), ())), preferred_element_type=F32)


def tn(a, b):
    return lax.dot_general(a, b, (((0,), (0,)), ((), ())), preferred_element_type=F32)


def comm_kernel(
    q_hbm, k_hbm, v_hbm, c_hbm, carry_hbm, gain_hbm,
    k, v, att, gq, gkp, gvp, suf, tot, gg,
    q, c, carry, gain,
    sb, rb, cb, ps, pre,
    sb2, rb2, cb2, ps2,
    zb, grow, gcol,
    sc_t, un, gu,
    in_sem, send_sem, recv_sem, tile_send, tile_recv,
):
    seq = lax.axis_index("seq")
    z = lax.axis_index("head")
    y = seq // ROW
    me = seq % ROW
    base = y * ROW

    def row_dev(kk):
        return (base + lax.rem(me + kk, ROW), z)

    def col_dev(kk):
        return (lax.rem(y + kk, COL) * ROW + me, z)

    def z_dev(kk):
        return (seq, lax.rem(z + kk, NZ))

    barrier = pltpu.get_barrier_semaphore()
    for dev, count in ((row_dev, ROW), (col_dev, COL), (z_dev, NZ)):
        for kk in range(1, count):
            pl.semaphore_signal(barrier, inc=1, device_id=dev(kk), device_id_type=MESH)

    loads = []
    for i, (src, dst) in enumerate(
        ((k_hbm, k), (v_hbm, v), (q_hbm, q), (c_hbm, c), (carry_hbm.at[me], carry), (gain_hbm, gain))
    ):
        load = pltpu.make_async_copy(src, dst, in_sem.at[i])
        load.start()
        loads.append(load)

    pending = []

    def exchange(sends, recvs, dev, count, src_of, dst_of, mine):
        for kk in FAR_FIRST:
            copy = pltpu.make_async_remote_copy(
                src_ref=src_of(lax.rem(mine + kk, count)),
                dst_ref=dst_of(mine),
                send_sem=sends.at[kk],
                recv_sem=recvs.at[kk],
                device_id=dev(kk),
                device_id_type=MESH,
            )
            copy.start()
            pending.append(copy)

        def wait():
            for kk in FAR_FIRST[::-1]:
                origin = lax.rem(mine + count - kk, count)
                pltpu.make_async_remote_copy(
                    src_ref=src_of(origin),
                    dst_ref=dst_of(origin),
                    send_sem=sends.at[kk],
                    recv_sem=recvs.at[kk],
                    device_id=dev(kk),
                    device_id_type=MESH,
                ).wait_recv()

        return wait

    def strip(n):
        return slice(n * PIECE, (n + 1) * PIECE)

    def piece(ref, i, n):
        return ref.at[i, pl.ds(n * PIECE, PIECE)]

    def scatter(stage, n, dev, count, src, dst, mine):
        return exchange(
            send_sem.at[stage, n], recv_sem.at[stage, n], dev, count,
            lambda t: piece(src, t, n), lambda t: piece(dst, t, n), mine,
        )

    def spread(stage, n, dev, count, ref, mine):
        return exchange(
            send_sem.at[stage, n], recv_sem.at[stage, n], dev, count,
            lambda t: piece(ref, mine, n), lambda t: piece(ref, t, n), mine,
        )

    def tiles(stage, dev, count, ref, mine):
        return exchange(
            tile_send.at[stage], tile_recv.at[stage], dev, count,
            lambda t: ref.at[mine], lambda t: ref.at[t], mine,
        )

    def head(ref, h):
        return ref[:, h * D:(h + 1) * D]

    rows = lax.broadcasted_iota(jnp.int32, (L, L), 0)
    cols = lax.broadcasted_iota(jnp.int32, (L, L), 1)
    lower = rows >= cols
    upper = rows <= cols

    loads[0].wait()
    loads[1].wait()
    for h in range(HEADS):
        state = tn(head(k, h), head(v, h)).astype(BF16)
        sb[2 * h] = state[:HALF]
        sb[2 * h + 1] = state[HALF:]
    pl.semaphore_wait(barrier, ROW + COL + NZ - 3)
    waits_a = [scatter(0, n, row_dev, ROW, sb, rb, me) for n in range(CHUNKS)]
    rb[me] = sb[me]

    loads[2].wait()
    for h in range(HEADS):
        score = jnp.where(lower, nt(head(q, h), head(k, h)), 0.0).astype(BF16)
        un[h] = nn(score, head(v, h))

    waits_b = []
    for n in range(CHUNKS):
        waits_a[n]()
        acc = rb[0, strip(n)].astype(F32)
        for r in range(1, ROW):
            acc = acc + rb[r, strip(n)].astype(F32)
        cb[y, strip(n)] = acc.astype(BF16)
        waits_b.append(spread(1, n, col_dev, COL, cb, y))

    for h in range(HEADS):
        sc_t[h] = jnp.where(upper, nt(head(k, h), head(q, h)), 0.0).astype(BF16)
    loads[3].wait()
    loads[4].wait()
    loads[5].wait()

    waits_c = []
    for n in range(CHUNKS):
        waits_b[n]()
        acc = carry[strip(n)]
        for r in range(COL):
            acc = acc + jnp.where(r < y, cb[r, strip(n)].astype(F32), 0.0)
        for r in range(ROW):
            ps[r, strip(n)] = acc.astype(BF16)
            if r < ROW - 1:
                acc = acc + rb[r, strip(n)].astype(F32)
        waits_c.append(scatter(2, n, row_dev, ROW, ps, pre, me))
    pre[me] = ps[me]
    for wait in waits_c:
        wait()

    square = jnp.zeros((L, D), F32)
    dots = jnp.zeros((L, D), F32)
    for h in range(HEADS):
        u = un[h] + nn(head(q, h), pre[2 * h:2 * h + 2].reshape(D, D))
        un[h] = u
        square = square + u * u
        dots = dots + head(c, h).astype(F32) * head(gain, h) * u

    def lane_sum(x):
        return jnp.sum(x.T, axis=0, keepdims=True)

    tile_row = lax.broadcasted_iota(jnp.int32, (8, D), 0)
    parts = (lane_sum(square[:D]), lane_sum(square[D:]), lane_sum(dots[:D]), lane_sum(dots[D:]))
    tile = jnp.zeros((8, D), F32)
    for i, part in enumerate(parts):
        tile = jnp.where(tile_row == i, part, tile)
    zb[z] = tile
    tiles(0, z_dev, NZ, zb, z)()
    sums = zb[0]
    for i in range(1, NZ):
        sums = sums + zb[i]
    mean = sums[0:2] / TOTAL_WIDTH + EPS
    inverse = 1.0 / jnp.sqrt(mean)
    factor = sums[2:4] / (TOTAL_WIDTH * mean)
    both = jnp.concatenate([inverse, factor, jnp.zeros((4, D), F32)], axis=0).T
    inv_col = jnp.concatenate([both[:, 0:1], both[:, 1:2]], axis=0)
    fac_col = jnp.concatenate([both[:, 2:3], both[:, 3:4]], axis=0)
    inv_col = jnp.broadcast_to(inv_col, (L, D))
    fac_col = jnp.broadcast_to(fac_col, (L, D))

    grow[me] = jnp.zeros((8, D), F32)
    for h in range(HEADS):
        cot = head(c, h).astype(F32)
        g = ((cot * head(gain, h) - un[h] * fac_col) * inv_col).astype(BF16)
        gu[h] = g
        state = tn(head(q, h), g).astype(BF16)
        sb2[2 * h] = state[:HALF]
        sb2[2 * h + 1] = state[HALF:]
    waits_a = [scatter(3, n, row_dev, ROW, sb2, rb2, me) for n in range(CHUNKS)]
    rb2[me] = sb2[me]

    for h in range(HEADS):
        normed = un[h] * inv_col
        att[:, h * D:(h + 1) * D] = (normed * head(gain, h)).astype(BF16)
        grow[me, h:h + 1] = jnp.sum(head(c, h).astype(F32) * normed, axis=0, keepdims=True)
    wait_g = tiles(1, row_dev, ROW, grow, me)

    waits_b = []
    for n in range(CHUNKS):
        waits_a[n]()
        acc = rb2[0, strip(n)].astype(F32)
        for r in range(1, ROW):
            acc = acc + rb2[r, strip(n)].astype(F32)
        cb2[y, strip(n)] = acc.astype(BF16)
        waits_b.append(spread(4, n, col_dev, COL, cb2, y))
    wait_g()
    gsum = grow[0]
    for r in range(1, ROW):
        gsum = gsum + grow[r]
    gcol[y] = gsum
    wait_g = tiles(2, col_dev, COL, gcol, y)

    for h in range(HEADS):
        lanes = slice(h * D, (h + 1) * D)
        mixed = jnp.where(lower, nt(gu[h], head(v, h)), 0.0).astype(BF16)
        gq[:, lanes] = (
            nn(mixed, head(k, h)) + nt(gu[h], pre[2 * h:2 * h + 2].reshape(D, D))
        ).astype(BF16)
        mixed_t = jnp.where(upper, nt(head(v, h), gu[h]), 0.0).astype(BF16)
        gkp[:, lanes] = nn(mixed_t, head(q, h))
        gvp[:, lanes] = nn(sc_t[h], gu[h])

    waits_c = []
    waits_t = []
    for n in range(CHUNKS):
        waits_b[n]()
        total = cb2[0, strip(n)].astype(F32)
        acc = jnp.zeros((PIECE, D), F32)
        for r in range(COL):
            row_sum = cb2[r, strip(n)].astype(F32)
            if r:
                total = total + row_sum
            acc = acc + jnp.where(r > y, row_sum, 0.0)
        for r in range(ROW - 1, -1, -1):
            ps2[r, strip(n)] = acc.astype(BF16)
            if r:
                acc = acc + rb2[r, strip(n)].astype(F32)
        waits_c.append(scatter(5, n, row_dev, ROW, ps2, suf, me))
        tot[me, strip(n)] = total.astype(BF16)
        waits_t.append(spread(6, n, row_dev, ROW, tot, me))
    suf[me] = ps2[me]
    wait_g()
    gsum = gcol[0]
    for r in range(1, COL):
        gsum = gsum + gcol[r]
    gg[...] = gsum
    for wait in waits_c + waits_t:
        wait()
    for copy in pending:
        copy.wait_send()


def tail_kernel(
    k, v, att, gq, gkp, gvp, suf, tot, gg,
    att_o, gq_o, gk_o, gv_o, gs_o, gain_o,
    gk, gv, gs, gain, sem,
):
    copies = []

    def store(src, dst):
        copy = pltpu.make_async_copy(src, dst, sem.at[len(copies)])
        copy.start()
        copies.append(copy)

    store(att, att_o)
    store(gq, gq_o)
    for h in range(HEADS):
        lanes = slice(h * D, (h + 1) * D)
        gk[:, lanes] = (gkp[:, lanes] + nt(v[:, lanes], suf[2 * h:2 * h + 2].reshape(D, D))).astype(BF16)
    store(gk, gk_o)
    for h in range(HEADS):
        lanes = slice(h * D, (h + 1) * D)
        gv[:, lanes] = (gvp[:, lanes] + nn(k[:, lanes], suf[2 * h:2 * h + 2].reshape(D, D))).astype(BF16)
    store(gv, gv_o)
    gs[...] = tot[...].astype(F32)
    store(gs, gs_o)
    for h in range(HEADS):
        gain[:, h * D:(h + 1) * D] = gg[h:h + 1]
    store(gain, gain_o)
    for copy in copies:
        copy.wait()


def on_device(queries, key_rows, values, cotangent, carried_state, norm_gain):
    any_spec = pl.BlockSpec(memory_space=pl.ANY)
    vmem_spec = pl.BlockSpec(memory_space=pltpu.VMEM)
    wide = (L, WIDTH)
    slices = (ROW, HALF, D)
    sds = jax.ShapeDtypeStruct
    vmem = pltpu.VMEM
    held = (
        vmem(wide, BF16), vmem(wide, BF16), vmem(wide, BF16), vmem(wide, BF16),
        vmem(wide, F32), vmem(wide, F32), vmem(slices, BF16), vmem(slices, BF16), vmem((8, D), F32),
    )
    parts = pl.pallas_call(
        comm_kernel,
        out_shape=held,
        in_specs=[pl.BlockSpec(memory_space=pltpu.HBM)] * 6,
        out_specs=[vmem_spec] * 9,
        scratch_shapes=[
            vmem(wide, BF16), vmem(wide, BF16), vmem((HALF, D), F32), vmem((1, WIDTH), F32),
            *[vmem(slices, BF16)] * 5,
            *[vmem(slices, BF16)] * 4,
            vmem((NZ, 8, D), F32), vmem((ROW, 8, D), F32), vmem((COL, 8, D), F32),
            vmem((HEADS, L, L), BF16), vmem((HEADS, L, D), F32), vmem((HEADS, L, D), BF16),
            pltpu.SemaphoreType.DMA((6,)),
            pltpu.SemaphoreType.DMA((7, CHUNKS, 8)), pltpu.SemaphoreType.DMA((7, CHUNKS, 8)),
            pltpu.SemaphoreType.DMA((3, 8)), pltpu.SemaphoreType.DMA((3, 8)),
        ],
        compiler_params=pltpu.CompilerParams(
            collective_id=0, has_side_effects=True, vmem_limit_bytes=16 * 2**20
        ),
        name="scan_comm",
    )(*[pltpu.with_memory_space_constraint(x, pltpu.HBM) for x in (queries, key_rows, values, cotangent, carried_state.reshape(slices), norm_gain.reshape(1, WIDTH))])
    att, gq, gk, gv, gs, gain = pl.pallas_call(
        tail_kernel,
        out_shape=(
            sds(wide, BF16), sds(wide, BF16), sds(wide, BF16), sds(wide, BF16),
            sds(slices, F32), sds((1, WIDTH), F32),
        ),
        in_specs=[vmem_spec] * 9,
        out_specs=[any_spec] * 6,
        scratch_shapes=[
            vmem(wide, BF16), vmem(wide, BF16), vmem(slices, F32), vmem((1, WIDTH), F32),
            pltpu.SemaphoreType.DMA((6,)),
        ],
        compiler_params=pltpu.CompilerParams(vmem_limit_bytes=16 * 2**20),
        name="tail",
    )(*parts)
    return att, gq, gk, gv, gs.reshape(HEADS, D, D), gain.reshape(WIDTH)


def solution(mesh):
    in_specs = (
        P("seq", "head"),
        P("seq", "head"),
        P("seq", "head"),
        P("seq", "head"),
        P("head", None, None),
        P("head"),
    )
    out_specs = (
        P("seq", "head"),
        P("seq", "head"),
        P("seq", "head"),
        P("seq", "head"),
        P("head", None, None),
        P("head"),
    )
    return jax.shard_map(
        on_device, mesh=mesh, in_specs=in_specs, out_specs=out_specs, check_vma=False
    )
```

time: 56.1 us -> 51.1 us (0.911)
  Pallas kernels: 55.3 us -> 50.3 us
    pallas_call x1, Pallas kernels: 52.4 us -> 49.1 us  [on_device(): pl.pallas_call(comm_kernel, out_shape=held, in_specs=[pl.BlockSpec(memory...]
    pallas_call x1, Pallas kernels: 2.88 us -> 1.17 us  [on_device(): pl.pallas_call(tail_kernel, out_shape=(sds(wide, BF16), sds(wide, BF16),...]
where the time goes in v2:
time: 51.1 us; the launch traced here: 50.9 us
  Pallas kernels  50.3 us (98%)
  between operations  0.64 us (1%)
    pallas_call x1, Pallas kernels, on_device(): pl.pallas_call(comm_kernel, out_shape=held, in_specs=[pl.BlockSpec(memory...  49.1 us
    pallas_call x1, Pallas kernels, on_device(): pl.pallas_call(tail_kernel, out_shape=(sds(wide, BF16), sds(wide, BF16),...  1.17 us

profile of v2, /device:TPU:1, one launch (start us, length us, event | category | flops | bytes accessed | tf_op | source)
XLA Modules:
  0.0 50.9 jit_solution(2084270091060691679)
XLA Ops:
  0.6 49.1 %scan_comm.1 = (bf16[256,512]{1,0:T(8,128)(2,1)S(1)}, bf16[256,512]{1,0:T(8,128)(2,1)S(1)}, bf16[256,512]{1,0:T(8,128)(2,1)S(1)}, bf16[256,512]{1,0:T(8,128)(2,1...) custom-call(bf16[256,512]{1,0:T(8,128)(2,1)} %q_hbm.1, ...), custom_call_target="tpu_custom_call" | custom-call | tf_op jit(solution)/shard_map/scan_comm/pallas_call | solution.py:326
  49.8 1.2 %tail.1 = (bf16[256,512]{1,0:T(8,128)(2,1)}, bf16[256,512]{1,0:T(8,128)(2,1)}, bf16[256,512]{1,0:T(8,128)(2,1)}, bf16[256,512]{1,0:T(8,128)(2,1)}, f32[8,64,128]{2,1,0:T(8,128)}, /*index=5*/f32[1,512]{1,0:T(1,128)}) custom-call(bf16[256,512]{1,0:T(8,128)(2,1)S(1)} %get-tuple-element.21.k, bf16[256,512]{1,0:T(8,128)(2,1)S(1)} %get-tuple-element.22.v, ...), custom_call_target="tpu_custom_call" | custom-call | tf_op jit(solution)/shard_map/tail/pallas_call | solution.py:346

commit v3 on v2

--- a/solution.py
+++ b/solution.py
@@ -18,6 +18,7 @@
 WIDTH = HEADS * D
 TOTAL_WIDTH = WIDTH * NZ
 HALF = D // 2
+TILE = 4
 CHUNKS = 1
 PIECE = HALF // CHUNKS
 FAR_FIRST = (4, 3, 5, 2, 6, 1, 7)
@@ -37,12 +38,12 @@
 
 def comm_kernel(
     q_hbm, k_hbm, v_hbm, c_hbm, carry_hbm, gain_hbm,
-    k, v, att, gq, gkp, gvp, suf, tot, gg,
-    q, c, carry, gain,
+    att, gq, gk, gv, tot, gg,
+    q, k, v, c, carry, gain,
     sb, rb, cb, ps, pre,
-    sb2, rb2, cb2, ps2,
+    sb2, rb2, cb2, ps2, suf,
     zb, grow, gcol,
-    sc_t, un, gu,
+    sc_t, un, gu, gkp, gvp,
     in_sem, send_sem, recv_sem, tile_send, tile_recv,
 ):
     seq = lax.axis_index("seq")
@@ -60,11 +61,6 @@
     def z_dev(kk):
         return (seq, lax.rem(z + kk, NZ))
 
-    barrier = pltpu.get_barrier_semaphore()
-    for dev, count in ((row_dev, ROW), (col_dev, COL), (z_dev, NZ)):
-        for kk in range(1, count):
-            pl.semaphore_signal(barrier, inc=1, device_id=dev(kk), device_id_type=MESH)
-
     loads = []
     for i, (src, dst) in enumerate(
         ((k_hbm, k), (v_hbm, v), (q_hbm, q), (c_hbm, c), (carry_hbm.at[me], carry), (gain_hbm, gain))
@@ -72,6 +68,11 @@
         load = pltpu.make_async_copy(src, dst, in_sem.at[i])
         load.start()
         loads.append(load)
+
+    barrier = pltpu.get_barrier_semaphore()
+    for dev, count in ((row_dev, ROW), (col_dev, COL), (z_dev, NZ)):
+        for kk in range(1, count):
+            pl.semaphore_signal(barrier, inc=1, device_id=dev(kk), device_id_type=MESH)
 
     pending = []
 
@@ -190,9 +191,9 @@
     def lane_sum(x):
         return jnp.sum(x.T, axis=0, keepdims=True)
 
-    tile_row = lax.broadcasted_iota(jnp.int32, (8, D), 0)
+    tile_row = lax.broadcasted_iota(jnp.int32, (TILE, D), 0)
     parts = (lane_sum(square[:D]), lane_sum(square[D:]), lane_sum(dots[:D]), lane_sum(dots[D:]))
-    tile = jnp.zeros((8, D), F32)
+    tile = jnp.zeros((TILE, D), F32)
     for i, part in enumerate(parts):
         tile = jnp.where(tile_row == i, part, tile)
     zb[z] = tile
@@ -209,7 +210,7 @@
     inv_col = jnp.broadcast_to(inv_col, (L, D))
     fac_col = jnp.broadcast_to(fac_col, (L, D))
 
-    grow[me] = jnp.zeros((8, D), F32)
+    grow[me] = jnp.zeros((TILE, D), F32)
     for h in range(HEADS):
         cot = head(c, h).astype(F32)
         g = ((cot * head(gain, h) - un[h] * fac_col) * inv_col).astype(BF16)
@@ -275,16 +276,23 @@
     for r in range(1, COL):
         gsum = gsum + gcol[r]
     gg[...] = gsum
-    for wait in waits_c + waits_t:
+    for wait in waits_c:
+        wait()
+    for h in range(HEADS):
+        lanes = slice(h * D, (h + 1) * D)
+        suffix = suf[2 * h:2 * h + 2].reshape(D, D)
+        gk[:, lanes] = (gkp[:, lanes] + nt(head(v, h), suffix)).astype(BF16)
+        gv[:, lanes] = (gvp[:, lanes] + nn(head(k, h), suffix)).astype(BF16)
+    for wait in waits_t:
         wait()
     for copy in pending:
         copy.wait_send()
 
 
 def tail_kernel(
-    k, v, att, gq, gkp, gvp, suf, tot, gg,
+    att, gq, gk, gv, tot, gg,
     att_o, gq_o, gk_o, gv_o, gs_o, gain_o,
-    gk, gv, gs, gain, sem,
+    gs, gain, sem,
 ):
     copies = []
 
@@ -295,13 +303,7 @@
 
     store(att, att_o)
     store(gq, gq_o)
-    for h in range(HEADS):
-        lanes = slice(h * D, (h + 1) * D)
-        gk[:, lanes] = (gkp[:, lanes] + nt(v[:, lanes], suf[2 * h:2 * h + 2].reshape(D, D))).astype(BF16)
     store(gk, gk_o)
-    for h in range(HEADS):
-        lanes = slice(h * D, (h + 1) * D)
-        gv[:, lanes] = (gvp[:, lanes] + nn(k[:, lanes], suf[2 * h:2 * h + 2].reshape(D, D))).astype(BF16)
     store(gv, gv_o)
     gs[...] = tot[...].astype(F32)
     store(gs, gs_o)
@@ -321,19 +323,20 @@
     vmem = pltpu.VMEM
     held = (
         vmem(wide, BF16), vmem(wide, BF16), vmem(wide, BF16), vmem(wide, BF16),
-        vmem(wide, F32), vmem(wide, F32), vmem(slices, BF16), vmem(slices, BF16), vmem((8, D), F32),
+        vmem(slices, BF16), vmem((TILE, D), F32),
     )
     parts = pl.pallas_call(
         comm_kernel,
         out_shape=held,
         in_specs=[pl.BlockSpec(memory_space=pltpu.HBM)] * 6,
-        out_specs=[vmem_spec] * 9,
+        out_specs=[vmem_spec] * 6,
         scratch_shapes=[
-            vmem(wide, BF16), vmem(wide, BF16), vmem((HALF, D), F32), vmem((1, WIDTH), F32),
+            *[vmem(wide, BF16)] * 4, vmem((HALF, D), F32), vmem((1, WIDTH), F32),
             *[vmem(slices, BF16)] * 5,
-            *[vmem(slices, BF16)] * 4,
-            vmem((NZ, 8, D), F32), vmem((ROW, 8, D), F32), vmem((COL, 8, D), F32),
+            *[vmem(slices, BF16)] * 5,
+            vmem((NZ, TILE, D), F32), vmem((ROW, TILE, D), F32), vmem((COL, TILE, D), F32),
             vmem((HEADS, L, L), BF16), vmem((HEADS, L, D), F32), vmem((HEADS, L, D), BF16),
+            vmem(wide, F32), vmem(wide, F32),
             pltpu.SemaphoreType.DMA((6,)),
             pltpu.SemaphoreType.DMA((7, CHUNKS, 8)), pltpu.SemaphoreType.DMA((7, CHUNKS, 8)),
             pltpu.SemaphoreType.DMA((3, 8)), pltpu.SemaphoreType.DMA((3, 8)),
@@ -349,10 +352,10 @@
             sds(wide, BF16), sds(wide, BF16), sds(wide, BF16), sds(wide, BF16),
             sds(slices, F32), sds((1, WIDTH), F32),
         ),
-        in_specs=[vmem_spec] * 9,
+        in_specs=[vmem_spec] * 6,
         out_specs=[any_spec] * 6,
         scratch_shapes=[
-            vmem(wide, BF16), vmem(wide, BF16), vmem(slices, F32), vmem((1, WIDTH), F32),
+            vmem(slices, F32), vmem((1, WIDTH), F32),
             pltpu.SemaphoreType.DMA((6,)),
         ],
         compiler_params=pltpu.CompilerParams(vmem_limit_bytes=16 * 2**20),

time: 51.1 us -> 50.7 us (level)
  no operation moved by 1% of the time
where the time goes in v3:
time: 50.7 us; the launch traced here: 50.5 us
  Pallas kernels  49.9 us (98%)
  between operations  0.64 us (1%)
    pallas_call x1, Pallas kernels, on_device(): pl.pallas_call(comm_kernel, out_shape=held, in_specs=[pl.BlockSpec(memory...  48.8 us
    pallas_call x1, Pallas kernels, on_device(): pl.pallas_call(tail_kernel, out_shape=(sds(wide, BF16), sds(wide, BF16),...  1.11 us

profile of v3, /device:TPU:1, one launch (start us, length us, event | category | flops | bytes accessed | tf_op | source)
XLA Modules:
  0.0 50.5 jit_solution(7509173896299002799)
XLA Ops:
  0.6 48.8 %scan_comm.1 = (bf16[256,512]{1,0:T(8,128)(2,1)S(1)}, bf16[256,512]{1,0:T(8,128)(2,1)S(1)}, bf16[256,512]{1,0:T(8,128)(2,1)S(1)}, bf16[256,512]{1,0:T(8,128)(2,1...) custom-call(bf16[256,512]{1,0:T(8,128)(2,1)} %q_hbm.1, bf16[256,512]{1,0:T(8,128)(2,1)} %k_hbm.1, ...), custom_call_target="tpu_custom_call" | custom-call | tf_op jit(solution)/shard_map/scan_comm/pallas_call | solution.py:328
  49.4 1.1 %tail.1 = (bf16[256,512]{1,0:T(8,128)(2,1)}, bf16[256,512]{1,0:T(8,128)(2,1)}, bf16[256,512]{1,0:T(8,128)(2,1)}, bf16[256,512]{1,0:T(8,128)(2,1)}, f32[8,64,128]{2,1,0:T(8,128)}, /*index=5*/f32[1,512]{1,0:T(1,128)}) custom-call(bf16[256,512]{1,0:T(8,128)(2,1)S(1)} %get-tuple-element.18.att, bf16[256,512]{1,0:T(8,128)(2,1)S(1)} %get-tuple-element.19.gq, ...), custom_call_target="tpu_custom_call" | custom-call | tf_op jit(solution)/shard_map/tail/pallas_call | solution.py:349

commit v4 on v3

--- a/solution.py
+++ b/solution.py
@@ -21,7 +21,7 @@
 TILE = 4
 CHUNKS = 1
 PIECE = HALF // CHUNKS
-FAR_FIRST = (4, 3, 5, 2, 6, 1, 7)
+FAR_FIRST = (4, 5, 3, 6, 2, 7, 1)
 
 
 def nn(a, b):

time: 50.7 us -> 50.4 us (level)
  no operation moved by 1% of the time
where the time goes in v4:
time: 50.4 us; the launch traced here: 50.3 us
  Pallas kernels  49.6 us (98%)
  between operations  0.64 us (1%)
    pallas_call x1, Pallas kernels, on_device(): pl.pallas_call(comm_kernel, out_shape=held, in_specs=[pl.BlockSpec(memory...  48.5 us
    pallas_call x1, Pallas kernels, on_device(): pl.pallas_call(tail_kernel, out_shape=(sds(wide, BF16), sds(wide, BF16),...  1.11 us

profile of v4, /device:TPU:1, one launch (start us, length us, event | category | flops | bytes accessed | tf_op | source)
XLA Modules:
  0.0 50.3 jit_solution(11036731269032854343)
XLA Ops:
  0.6 48.5 %scan_comm.1 = (bf16[256,512]{1,0:T(8,128)(2,1)S(1)}, bf16[256,512]{1,0:T(8,128)(2,1)S(1)}, bf16[256,512]{1,0:T(8,128)(2,1)S(1)}, bf16[256,512]{1,0:T(8,128)(2,1...) custom-call(bf16[256,512]{1,0:T(8,128)(2,1)} %q_hbm.1, bf16[256,512]{1,0:T(8,128)(2,1)} %k_hbm.1, ...), custom_call_target="tpu_custom_call" | custom-call | tf_op jit(solution)/shard_map/scan_comm/pallas_call | solution.py:328
  49.2 1.1 %tail.1 = (bf16[256,512]{1,0:T(8,128)(2,1)}, bf16[256,512]{1,0:T(8,128)(2,1)}, bf16[256,512]{1,0:T(8,128)(2,1)}, bf16[256,512]{1,0:T(8,128)(2,1)}, f32[8,64,128]{2,1,0:T(8,128)}, /*index=5*/f32[1,512]{1,0:T(1,128)}) custom-call(bf16[256,512]{1,0:T(8,128)(2,1)S(1)} %get-tuple-element.18.att, bf16[256,512]{1,0:T(8,128)(2,1)S(1)} %get-tuple-element.19.gq, ...), custom_call_target="tpu_custom_call" | custom-call | tf_op jit(solution)/shard_map/tail/pallas_call | solution.py:349
